TPU v7x, 256 devices: a whole 4x4x8 slice. The times are simulated.
256 devices in a mesh: ctx: 8 (over x, y_lo), chan: 32 (over y_hi, z, core).
Axes of the slice: x: 4, y: 4 (y_hi: 2, y_lo: 2; y = y_hi * 2 + y_lo), z: 8, core: 2. Of those that a mesh axis runs over, the one named last changes fastest.
Arguments:
- tokens: bfloat16 [4096, 8192], P('ctx', 'chan'), may hold values from -6 to 6
- in_base: bfloat16 [8192, 3, 4096], P('ctx', None, 'chan'), may hold values from -0.0625 to 0.0625
- in_task: bfloat16 [8192, 3, 4096], P('ctx', None, 'chan'), may hold values from -0.03125 to 0.03125
- feat_weight: float32 [7, 3, 4096], P(None, None, 'chan'), may hold values from -2 to 2
- filter_taps: float32 [128, 4096], P(None, 'chan'), may hold values from -0.5 to 0.5
- decay_rates: float32 [4096], P('chan'), may hold values from 0.002 to 0.08
- skip_gain: float32 [4096], P('chan'), may hold values from -1 to 1
- out_base: bfloat16 [4096, 8192], P('chan', 'ctx'), may hold values from -0.1875 to 0.1875
- out_task: bfloat16 [4096, 8192], P('chan', 'ctx'), may hold values from -0.046875 to 0.046875
Outputs:
- layer_out: bfloat16 [4096, 8192], P('ctx', 'chan')
All inputs are finite; a program needn't handle non-finite values.
Results may differ from a plain program's by a relative error of at most 0.0092.
Values may be sent and summed in bfloat16 or wider, within the bound.
A program may use at most 128 MiB of HBM per device.

v0:
```python
import jax
import jax.numpy as jnp
from jax import lax
from jax.sharding import PartitionSpec as P


def shifted(value, axis, by):
    size = lax.axis_size(axis)
    pairs = [(i, i + by) for i in range(size) if 0 <= i + by < size]
    return lax.ppermute(value, axis, pairs)


def featurize_valid(extended, feat_weight, count):
    taps_short = feat_weight.shape[0]
    result = jnp.zeros((count,) + extended.shape[1:], jnp.float32)
    for offset in range(taps_short):
        begin_at = taps_short - 1 - offset
        result = result + feat_weight[offset] * extended[begin_at : begin_at + count].astype(
            jnp.float32
        )
    return result


def negate_task(base_part, task_part):
    return (base_part.astype(jnp.float32) - task_part.astype(jnp.float32)).astype(jnp.bfloat16)


def shards(
    tokens, in_base, in_task, feat_weight, filter_taps, decay_rates, skip_gain, out_base, out_task
):
    base_all, task_all = (
        lax.all_gather(in_base, "ctx", axis=0, tiled=True),
        lax.all_gather(in_task, "ctx", axis=0, tiled=True),
    )
    in_weight = negate_task(base_all, task_all)
    width_all = in_weight.shape[0]
    chan_local = in_weight.shape[2]
    flat_weight = in_weight.reshape(width_all, 3 * chan_local)
    tok_rows = tokens.shape[0]
    projected = jnp.dot(
        lax.all_gather(tokens, "chan", axis=1, tiled=True),
        flat_weight,
        preferred_element_type=jnp.float32,
    )
    projected = projected.astype(jnp.bfloat16).reshape(tok_rows, 3, chan_local)
    taps_long = filter_taps.shape[0]
    taps_short = feat_weight.shape[0]
    lag_values = jnp.arange(taps_long, dtype=jnp.float32)
    filter_full = filter_taps * jnp.exp(-decay_rates[None, :] * lag_values[:, None])
    rim_rows = shifted(projected[tok_rows - (taps_short - 1) :], "ctx", 1)
    extended = jnp.concatenate([rim_rows, projected], axis=0)
    featured = featurize_valid(extended, feat_weight, tok_rows)
    query_part = featured[:, 0, :]
    own_input = featured[:, 1, :] * featured[:, 2, :]
    input_rim = shifted(own_input[tok_rows - (taps_long - 1) :], "ctx", 1)
    long_input = jnp.concatenate([input_rim, own_input], axis=0)
    mixed = skip_gain * own_input
    conv_sum = jnp.zeros((tok_rows, chan_local), jnp.float32)
    for lag_index in range(taps_long):
        begin_at = taps_long - 1 - lag_index
        conv_sum = conv_sum + filter_full[lag_index] * long_input[begin_at : begin_at + tok_rows]
    mixed = mixed + conv_sum
    gated_out = (query_part * mixed).astype(jnp.bfloat16)
    base_cols, task_cols = (
        lax.all_gather(out_base, "ctx", axis=1, tiled=True),
        lax.all_gather(out_task, "ctx", axis=1, tiled=True),
    )
    out_weight = negate_task(base_cols, task_cols)
    partial_terms = jnp.dot(gated_out, out_weight, preferred_element_type=jnp.float32)
    summed = lax.psum_scatter(partial_terms, "chan", scatter_dimension=1, tiled=True)
    return summed.astype(jnp.bfloat16)


def solution(mesh):
    in_specs = (
        P("ctx", "chan"),
        P("ctx", None, "chan"),
        P("ctx", None, "chan"),
        P(None, None, "chan"),
        P(None, "chan"),
        P("chan"),
        P("chan"),
        P("chan", "ctx"),
        P("chan", "ctx"),
    )
    out_specs = P("ctx", "chan")
    return jax.shard_map(shards, mesh=mesh, in_specs=in_specs, out_specs=out_specs, check_vma=False)
```

profile of v0, /device:TPU:4, one launch (start us, length us, event | category | flops | bytes accessed | tf_op | source)
XLA Modules:
  0.0 755.3 jit_solution(2563523671187403728)
XLA Ops:
  6.5 2.3 copy.10
  8.9 2.3 copy.11
  11.3 0.7 all-gather.10.cloned.1.call-update
  12.0 0.5 all-gather.12.cloned.1.call-update
  12.6 0.5 all-gather.14.cloned.1.call-update
  13.2 0.7 neg.4
  13.9 0.9 exponential_multiply_fusion
  14.9 1.0 fusion.391
  15.9 127.7 %all-gather.6.cloned.1.call-done = bf16[8192,3,128]{0,2,1:T(8,128)(2,1)} async-done(((bf16[1024,3,128]{0,2,1:T(8,128)(2,1)}), bf16[8192,3,128]{0,2,1:T(8,128)(2,1)}) %all-gather.6.cloned.1.call-update) | async-done | bytes 6291472 | tf_op jit(solution)/shard_map/all_gather | solution.py:32
  143.6 134.7 %all-gather.8.cloned.1.call-done = bf16[8192,3,128]{0,2,1:T(8,128)(2,1)} async-done(((bf16[1024,3,128]{0,2,1:T(8,128)(2,1)}), bf16[8192,3,128]{0,2,1:T(8,128)(2,1)}) %all-gather.8.cloned.1.call-update) | async-done | bytes 6291472 | tf_op jit(solution)/shard_map/all_gather | solution.py:33
  278.4 9.9 %subtract_convert_fusion = bf16[8192,3,128]{0,2,1:T(8,128)(2,1)} fusion(bf16[8192,3,128]{0,2,1:T(8,128)(2,1)} %all-gather.8.cloned.1.call-done, bf16[8192,3,128]{0,2,1:T(8,128)(2,1)} %all-gather.6.cloned.1.call-done), kind=kLoop, calls=%fused_computation.126 | loop fusion | flops 12582912 | bytes 18874368 | tf_op jit(solution)/shard_map/convert_element_type | solution.py:25
  288.3 102.3 %all-gather.10.cloned.1.call-done = bf16[512,8192]{1,0:T(8,128)(2,1)} async-done(((bf16[512,256]{1,0:T(8,128)(2,1)}), bf16[512,8192]{1,0:T(8,128)(2,1)}) %all-gather.10.cloned.1.call-update) | async-done | bytes 8388624 | tf_op jit(solution)/shard_map/all_gather | solution.py:41
  390.5 8.6 %convolution_convert_fusion = bf16[384,512]{1,0:T(8,128)(2,1)S(1)} fusion(bf16[8192,384]{0,1:T(8,128)(2,1)} %bitcast.287, bf16[512,8192]{1,0:T(8,128)(2,1)} %all-gather.10.cloned.1.call-done), kind=kOutput, calls=%fused_computation.255 | convolution fusion | flops 3221422080 | bytes 15073280 | tf_op jit(solution)/shard_map/dot_general | solution.py:40
  399.2 0.1 slice.1100
  399.3 2.5 collective-permute-start
  401.8 6.1 collective-permute-done
  407.9 1.5 multiply_add_fusion
  409.4 0.1 slice_bitcast_fusion.1
  409.5 4.6 collective-permute-start.1
  414.1 32.5 %all-gather.12.cloned.1.call-done = bf16[128,8192]{1,0:T(8,128)(2,1)} async-done(((bf16[128,1024]{1,0:T(8,128)(2,1)}), bf16[128,8192]{1,0:T(8,128)(2,1)}) %all-gather.12.cloned.1.call-update) | async-done | bytes 2097168 | tf_op jit(solution)/shard_map/all_gather | solution.py:65
  446.6 55.2 %all-gather.14.cloned.1.call-done = bf16[128,8192]{1,0:T(8,128)(2,1)} async-done(((bf16[128,1024]{1,0:T(8,128)(2,1)}), bf16[128,8192]{1,0:T(8,128)(2,1)}) %all-gather.14.cloned.1.call-update) | async-done | bytes 2097168 | tf_op jit(solution)/shard_map/all_gather | solution.py:66
  501.8 23.9 %fusion = f32[512,8192]{1,0:T(8,128)} fusion(bf16[128,8192]{1,0:T(8,128)(2,1)} %all-gather.14.cloned.1.call-done, bf16[128,8192]{1,0:T(8,128)(2,1)} %all-gather.12.cloned.1.call-done, f32[512,128]{0,1:T(8,128)S(1)} %fusion.394, f32[127,128]{0,1:T(8,128)S(1)} %collective-permute-done.1, f32[512,3,128]{0,2,1:T(8,128)S(1)} %multiply_add_fusion, ...), kind=kOutput, calls=%fused_computation.128 | convolution fusion | flops 1103233024 | bytes 21627392 | tf_op jit(solution)/shard_map/dot_general | solution.py:69
  525.7 221.0 %reduce-scatter.2.cloned.1.call-done = f32[512,256]{1,0:T(8,128)} async-done(((f32[512,8192]{1,0:T(8,128)}), f32[512,256]{1,0:T(8,128)}) %reduce-scatter.2.cloned.1.call-update) | async-done | bytes 524304 | tf_op jit(solution)/shard_map/reduce_scatter | solution.py:70
  746.7 1.8 convert_element_type.67
  (25 shorter events, 0.4 us)
Async XLA Ops:
  6.5 137.1 %all-gather.6.cloned.1.call-start = ((), (), s32[]{:S(2)}) async-start(), calls=%async_computation.1 | async-start | bytes 7077888 | tf_op jit(solution)/shard_map/all_gather | solution.py:32
  8.9 269.5 %all-gather.8.cloned.1.call-start = ((), (), s32[]{:S(2)}) async-start(), calls=%async_computation.2 | async-start | bytes 7077888 | tf_op jit(solution)/shard_map/all_gather | solution.py:33
  11.3 379.3 %all-gather.10.cloned.1.call-start = ((), (), s32[]{:S(2)}) async-start(), calls=%async_computation.3 | async-start | bytes 8650752 | tf_op jit(solution)/shard_map/all_gather | solution.py:41
  12.0 434.6 %all-gather.12.cloned.1.call-start = ((), (), s32[]{:S(2)}) async-start(), calls=%async_computation.4 | async-start | bytes 2359296 | tf_op jit(solution)/shard_map/all_gather | solution.py:65
  12.6 489.2 %all-gather.14.cloned.1.call-start = ((), (), s32[]{:S(2)}) async-start(), calls=%async_computation.5 | async-start | bytes 2359296 | tf_op jit(solution)/shard_map/all_gather | solution.py:66
  13.2 733.5 %reduce-scatter.2.cloned.1.call-start = ((), (), s32[]{:S(2)}) async-start(), calls=%async_computation.6 | async-start | bytes 17301504 | tf_op jit(solution)/shard_map/reduce_scatter | solution.py:70
  390.5 111.3 %copy-start = (f32[128]{0:T(128)S(1)}, f32[128]{0:T(128)}, u32[]{:S(2)}) copy-start(f32[128]{0:T(128)} %param.15) | copy-start | bytes 1540
  399.3 8.6 %collective-permute-start = (bf16[6,3,128]{0,2,1:T(8,128)(2,1)S(1)}, bf16[6,3,128]{0,2,1:T(8,128)(2,1)S(1)}, u32[]{:S(2)}, u32[]{:S(2)}) collective-permute-start(bf16[6,3,128]{0,2,1:T(8,128)(2,1)S(1)} %bitcast.290), channel_id=1, source_target_pairs={{0,32},{32,64},{64,96},{96,128},{128,160},{160,192},{192,224},{1,3... | collective-permute-start | bytes 13832 | tf_op jit(solution)/shard_map/ppermute | solution.py:10
  409.5 92.3 %collective-permute-start.1 = (f32[127,128]{0,1:T(8,128)S(1)}, f32[127,128]{0,1:T(8,128)S(1)}, u32[]{:S(2)}, u32[]{:S(2)}) collective-permute-start(f32[127,128]{0,1:T(8,128)S(1)} %slice_bitcast_fusion.1), channel_id=1, source_target_pairs={{0,32},{32,64},{64,96},{96,128},{128,160},{160,192},{192,224},{1,3... | collective-permute-start | bytes 195080 | tf_op jit(solution)/shard_map/ppermute | solution.py:10
Sparse Core Ops, SparseCore 0:
  9.1 134.4 all-gather.5
  145.4 132.9 all-gather.7
  280.9 109.5 all-gather.9
  392.2 54.3 all-gather.11
  448.2 53.5 all-gather.13
  525.8 220.7 reduce-scatter.1
where the time goes:
time: 756 us; the launch traced here: 755 us
  waiting for transfers between devices  681 us (90%)
  matrix products  32.5 us (4%)
  other arithmetic  14.8 us (2%)
  between operations  13.6 us (2%)
    reduce_scatter x1, waiting for transfers between devices, shards(): lax.psum_scatter(partial_terms, 'chan', scatter_dimension=1, tiled=True)  221 us
    all_gather x1, waiting for transfers between devices, shards(): lax.all_gather(in_task, 'ctx', axis=0, tiled=True)  135 us
    all_gather x1, waiting for transfers between devices, shards(): lax.all_gather(in_base, 'ctx', axis=0, tiled=True)  128 us
    all_gather x1, waiting for transfers between devices, shards(): lax.all_gather(tokens, 'chan', axis=1, tiled=True)  102 us
    all_gather x1, waiting for transfers between devices, shards(): lax.all_gather(out_task, 'ctx', axis=1, tiled=True)  55.2 us
    all_gather x1, waiting for transfers between devices, shards(): lax.all_gather(out_base, 'ctx', axis=1, tiled=True)  32.5 us
    dot_general x1, matrix products, shards(): jnp.dot(gated_out, out_weight, preferred_element_type=jnp.float32)  23.9 us
  transfers between devices with their start and end apart: 8, of which 7 were waited for; matrix products, arithmetic and copies ran while one was open for 3% of the time, Pallas kernels for 0%

commit v1 on v0

--- a/solution.py
+++ b/solution.py
@@ -29,7 +29,9 @@
     tokens, in_base, in_task, feat_weight, filter_taps, decay_rates, skip_gain, out_base, out_task
 ):
     base_all, task_all = (
-        lax.all_gather(in_base, "ctx", axis=0, tiled=True),
+        jnp.concatenate(
+            lax.all_to_all(jnp.stack([in_base] * lax.axis_size("ctx")), "ctx", 0, 0), axis=0
+        ),
         lax.all_gather(in_task, "ctx", axis=0, tiled=True),
     )
     in_weight = negate_task(base_all, task_all)

time: 756 us -> 688 us (0.910)
  waiting for transfers between devices: 681 us -> 585 us
  local copies, waits for them, and re-layouts: 5.88 us -> 19.2 us
  other arithmetic: 14.8 us -> 23.3 us
    all_gather x1 -> x0, waiting for transfers between devices: 128 us -> none  [shards(): lax.all_gather(in_base, 'ctx', axis=0, tiled=True)]
    all_to_all x0 -> x1, waiting for transfers between devices: none -> 107 us  [shards(): lax.all_to_all(jnp.stack([in_base] * lax.axis_size('ctx')), 'ctx', 0, 0)]
    all_gather x1, waiting for transfers between devices: 135 us -> 57.6 us  [shards(): lax.all_gather(in_task, 'ctx', axis=0, tiled=True)]
    all_gather x1, waiting for transfers between devices: 32.5 us -> 55.4 us  [shards(): lax.all_gather(out_base, 'ctx', axis=1, tiled=True)]
    all_gather x1, waiting for transfers between devices: 55.2 us -> 32.5 us  [shards(): lax.all_gather(out_task, 'ctx', axis=1, tiled=True)]
    convert_element_type x0 -> x1, local copies, waits for them, and re-layouts: none -> 11.8 us  [negate_task(): base_part.astype(jnp.float32) - task_part.astype(jnp.float32)]
    unnamed x0 -> x1, other arithmetic: none -> 8.94 us
  transfers between devices with their start and end apart: 8 -> 8, of which waited for: 7 -> 7; matrix products, arithmetic and copies ran while one was open for 3% -> 7% of each run, Pallas kernels for 0% -> 0%
where the time goes in v1:
time: 688 us; the launch traced here: 687 us
  waiting for transfers between devices  585 us (85%)
  matrix products  32.5 us (5%)
  other arithmetic  23.3 us (3%)
  local copies, waits for them, and re-layouts  19.2 us (3%)
  starting transfers between devices  14.2 us (2%)
  between operations  13.3 us (2%)
    reduce_scatter x1, waiting for transfers between devices, shards(): lax.psum_scatter(partial_terms, 'chan', scatter_dimension=1, tiled=True)  221 us
    all_to_all x1, waiting for transfers between devices, shards(): lax.all_to_all(jnp.stack([in_base] * lax.axis_size('ctx')), 'ctx', 0, 0)  107 us
    all_gather x1, waiting for transfers between devices, shards(): lax.all_gather(tokens, 'chan', axis=1, tiled=True)  103 us
    all_gather x1, waiting for transfers between devices, shards(): lax.all_gather(in_task, 'ctx', axis=0, tiled=True)  57.6 us
    all_gather x1, waiting for transfers between devices, shards(): lax.all_gather(out_base, 'ctx', axis=1, tiled=True)  55.4 us
    all_gather x1, waiting for transfers between devices, shards(): lax.all_gather(out_task, 'ctx', axis=1, tiled=True)  32.5 us
    dot_general x1, matrix products, shards(): jnp.dot(gated_out, out_weight, preferred_element_type=jnp.float32)  23.9 us
  transfers between devices with their start and end apart: 8, of which 7 were waited for; matrix products, arithmetic and copies ran while one was open for 7% of the time, Pallas kernels for 0%

profile of v1, /device:TPU:4, one launch (start us, length us, event | category | flops | bytes accessed | tf_op | source)
XLA Modules:
  0.0 687.4 jit_solution(3188731824433206268)
XLA Ops:
  6.5 2.3 copy.14
  8.9 0.7 all-gather.7.cloned.1.call-update
  9.6 0.7 all-gather.11.cloned.1.call-update
  10.3 1.4 copy.12
  11.7 3.4 stack.2
  15.2 7.0 %all-to-all-start = ((bf16[8,1024,3,128]{1,3,2,0:T(8,128)(2,1)}), bf16[8,1024,3,128]{1,3,2,0:T(8,128)(2,1)}, u32[]{:S(2)}, u32[]{:S(2)}) async-start(bf16[8,1024,3,128]{1,3,2,0:T(8,128)(2,1)} %stack.2), calls=%async_computation | async-start | bytes 12582912 | tf_op jit(solution)/shard_map/all_to_all | solution.py:33
  22.2 0.6 all-gather.9.cloned.1.call-update
  23.1 107.4 %all-to-all-done = bf16[8,1024,3,128]{1,3,2,0:T(8,128)(2,1)} async-done(((bf16[8,1024,3,128]{1,3,2,0:T(8,128)(2,1)}), bf16[8,1024,3,128]{1,3,2,0:T(8,128)(2,1)}, u32[]{:S(2)}, u32[]{:S(2)}) %all-to-all-start) | async-done | bytes 6291488 | tf_op jit(solution)/shard_map/all_to_all | solution.py:33
  130.4 8.9 %convert_bitcast_fusion = f32[8,3,16,8,1024]{4,3,2,1,0:T(8,128)} fusion(bf16[8,1024,3,128]{1,3,2,0:T(8,128)(2,1)} %all-to-all-done), kind=kLoop, calls=%fused_computation.126 | loop fusion | flops 3145728 | bytes 18874368
  139.4 11.8 %copy.22 = f32[8,3,16,8,1024]{4,3,0,2,1:T(8,128)} copy(f32[8,3,16,8,1024]{4,3,2,1,0:T(8,128)} %convert_bitcast_fusion) | data formatting | bytes 25165824 | tf_op jit(solution)/shard_map/convert_element_type | solution.py:25
  151.2 57.6 %all-gather.5.cloned.1.call-done = bf16[8192,3,128]{0,2,1:T(8,128)(2,1)} async-done(((bf16[1024,3,128]{0,2,1:T(8,128)(2,1)}), bf16[8192,3,128]{0,2,1:T(8,128)(2,1)}) %all-gather.5.cloned.1.call-update) | async-done | bytes 6291472 | tf_op jit(solution)/shard_map/all_gather | solution.py:35
  208.9 11.0 %subtract_convert_fusion = bf16[8192,3,128]{0,2,1:T(8,128)(2,1)} fusion(f32[8192,3,128]{0,2,1:T(8,128)} %bitcast.290, bf16[8192,3,128]{0,2,1:T(8,128)(2,1)} %all-gather.5.cloned.1.call-done), kind=kLoop, calls=%fused_computation.127 | loop fusion | flops 9437184 | bytes 25165824 | tf_op jit(solution)/shard_map/convert_element_type | solution.py:25
  219.8 102.8 %all-gather.7.cloned.1.call-done = bf16[512,8192]{1,0:T(8,128)(2,1)} async-done(((bf16[512,256]{1,0:T(8,128)(2,1)}), bf16[512,8192]{1,0:T(8,128)(2,1)}) %all-gather.7.cloned.1.call-update) | async-done | bytes 8388624 | tf_op jit(solution)/shard_map/all_gather | solution.py:43
  322.6 8.6 %convolution_convert_fusion = bf16[384,512]{1,0:T(8,128)(2,1)S(1)} fusion(bf16[8192,384]{0,1:T(8,128)(2,1)} %bitcast.291, bf16[512,8192]{1,0:T(8,128)(2,1)} %all-gather.7.cloned.1.call-done), kind=kOutput, calls=%fused_computation.256 | convolution fusion | flops 3221422080 | bytes 15073280 | tf_op jit(solution)/shard_map/dot_general | solution.py:42
  331.3 0.1 slice.1100
  331.4 2.5 collective-permute-start
  333.9 6.2 collective-permute-done
  340.1 1.5 multiply_add_fusion
  341.7 4.6 collective-permute-start.1
  346.3 32.5 %all-gather.11.cloned.1.call-done = bf16[128,8192]{1,0:T(8,128)(2,1)} async-done(((bf16[128,1024]{1,0:T(8,128)(2,1)}), bf16[128,8192]{1,0:T(8,128)(2,1)}) %all-gather.11.cloned.1.call-update) | async-done | bytes 2097168 | tf_op jit(solution)/shard_map/all_gather | solution.py:68
  378.8 55.4 %all-gather.9.cloned.1.call-done = bf16[128,8192]{1,0:T(8,128)(2,1)} async-done(((bf16[128,1024]{1,0:T(8,128)(2,1)}), bf16[128,8192]{1,0:T(8,128)(2,1)}) %all-gather.9.cloned.1.call-update) | async-done | bytes 2097168 | tf_op jit(solution)/shard_map/all_gather | solution.py:67
  434.2 23.9 %fusion = f32[512,8192]{1,0:T(8,128)} fusion(bf16[128,8192]{1,0:T(8,128)(2,1)} %all-gather.11.cloned.1.call-done, bf16[128,8192]{1,0:T(8,128)(2,1)} %all-gather.9.cloned.1.call-done, f32[512,128]{0,1:T(8,128)S(1)} %fusion.394, f32[127,128]{0,1:T(8,128)S(1)} %collective-permute-done.1, f32[512,3,128]{0,2,1:T(8,128)S(1)} %multiply_add_fusion, ...), kind=kOutput, calls=%fused_computation.129 | convolution fusion | flops 1103233024 | bytes 21627392 | tf_op jit(solution)/shard_map/dot_general | solution.py:71
  458.1 220.9 %reduce-scatter.2.cloned.1.call-done = f32[512,256]{1,0:T(8,128)} async-done(((f32[512,8192]{1,0:T(8,128)}), f32[512,256]{1,0:T(8,128)}) %reduce-scatter.2.cloned.1.call-update) | async-done | bytes 524304 | tf_op jit(solution)/shard_map/reduce_scatter | solution.py:72
  679.1 1.8 convert_element_type.71
  (33 shorter events, 0.5 us)
Async XLA Ops:
  6.5 202.3 %all-gather.5.cloned.1.call-start = ((), (), s32[]{:S(2)}) async-start(), calls=%async_computation.2 | async-start | bytes 7077888 | tf_op jit(solution)/shard_map/all_gather | solution.py:35
  8.8 313.8 %all-gather.7.cloned.1.call-start = ((), (), s32[]{:S(2)}) async-start(), calls=%async_computation.3 | async-start | bytes 8650752 | tf_op jit(solution)/shard_map/all_gather | solution.py:43
  9.6 369.3 %all-gather.11.cloned.1.call-start = ((), (), s32[]{:S(2)}) async-start(), calls=%async_computation.5 | async-start | bytes 2359296 | tf_op jit(solution)/shard_map/all_gather | solution.py:68
  15.2 7.6 %copy-start.2 = (f32[128]{0:T(128)S(1)}, f32[128]{0:T(128)}, u32[]{:S(2)}) copy-start(f32[128]{0:T(128)} %param.14) | copy-start | bytes 1540
  15.2 7.6 %copy-start.1 = (f32[7,3,128]{2,0,1:T(8,128)S(1)}, f32[7,3,128]{2,0,1:T(8,128)}, u32[]{:S(2)}) copy-start(f32[7,3,128]{2,0,1:T(8,128)} %param.12) | copy-start | bytes 32260
  15.2 7.7 %copy-start = (f32[128,128]{1,0:T(8,128)S(1)}, f32[128,128]{1,0:T(8,128)}, u32[]{:S(2)}) copy-start(f32[128,128]{1,0:T(8,128)} %param.13) | copy-start | bytes 196612
  15.2 115.3 %all-to-all-start = ((bf16[8,1024,3,128]{1,3,2,0:T(8,128)(2,1)}), bf16[8,1024,3,128]{1,3,2,0:T(8,128)(2,1)}, u32[]{:S(2)}, u32[]{:S(2)}) async-start(bf16[8,1024,3,128]{1,3,2,0:T(8,128)(2,1)} %stack.2), calls=%async_computation | async-start | bytes 12582912 | tf_op jit(solution)/shard_map/all_to_all | solution.py:33
  22.2 412.0 %all-gather.9.cloned.1.call-start = ((), (), s32[]{:S(2)}) async-start(), calls=%async_computation.4 | async-start | bytes 2359296 | tf_op jit(solution)/shard_map/all_gather | solution.py:67
  22.7 656.3 %reduce-scatter.2.cloned.1.call-start = ((), (), s32[]{:S(2)}) async-start(), calls=%async_computation.6 | async-start | bytes 17301504 | tf_op jit(solution)/shard_map/reduce_scatter | solution.py:72
  322.6 111.6 %copy-start.3 = (f32[128]{0:T(128)S(1)}, f32[128]{0:T(128)}, u32[]{:S(2)}) copy-start(f32[128]{0:T(128)} %param.15) | copy-start | bytes 1540
  331.4 8.7 %collective-permute-start = (bf16[6,3,128]{0,2,1:T(8,128)(2,1)S(1)}, bf16[6,3,128]{0,2,1:T(8,128)(2,1)S(1)}, u32[]{:S(2)}, u32[]{:S(2)}) collective-permute-start(bf16[6,3,128]{0,2,1:T(8,128)(2,1)S(1)} %bitcast.294), channel_id=1, source_target_pairs={{0,32},{32,64},{64,96},{96,128},{128,160},{160,192},{192,224},{1,3... | collective-permute-start | bytes 13832 | tf_op jit(solution)/shard_map/ppermute | solution.py:10
  341.7 92.5 %collective-permute-start.1 = (f32[127,128]{0,1:T(8,128)S(1)}, f32[127,128]{0,1:T(8,128)S(1)}, u32[]{:S(2)}, u32[]{:S(2)}) collective-permute-start(f32[127,128]{0,1:T(8,128)S(1)} %slice_bitcast_fusion.1), channel_id=1, source_target_pairs={{0,32},{32,64},{64,96},{96,128},{128,160},{160,192},{192,224},{1,3... | collective-permute-start | bytes 195080 | tf_op jit(solution)/shard_map/ppermute | solution.py:10
Sparse Core Ops, SparseCore 0:
  9.1 199.6 all-gather.4
  211.4 111.1 all-gather.6
  324.4 54.3 all-gather.10
  380.5 53.6 all-gather.8
  458.3 220.7 reduce-scatter.1
